TPU v7x, 256 devices: a whole 4x4x8 slice. The times are simulated.
256 devices in a mesh: row: 8 (over z), col: 32 (over y, x, core).
Axes of the slice: x: 4, y: 4, z: 8, core: 2. Of those that a mesh axis runs over, the one named last changes fastest.
Arguments:
- point_data: float32 [4, 65536], P(None, ('row', 'col')), may hold values from 0 to 32, as said below
- right_side: float32 [64, 65536], P(None, ('row', 'col')), may hold values from -45 to 45
- pair_list: int32 [2, 4444], replicated, may hold values from 0 to 511, as said below
Outputs:
- solution: float32 [64, 65536], P(None, ('row', 'col'))
- residual: float32 [64, 65536], P(None, ('row', 'col'))
Inputs may be any that keep to these rules, and one draw needn't show every extreme that they name: `point_data`: the points of block b lie in one unit cell of a 4 x 4 x 32 grid, one block to a cell; row 3 lies in 0.2 to 0.6. `pair_list`: each column (I, J) has I < J and names two blocks whose cells lie within one cell of each other along every dimension; every such pair is listed exactly once. The columns stand grouped by the device (I // 2 // 32, (J // 2) % 32) of the row and col axes, groups in row-major order.
All inputs are finite; a program needn't handle non-finite values.
Results may differ from a plain program's by a relative error of at most 0.018.
Values may be sent and summed in bfloat16 or wider, within the bound.
A program may use at most 64 MiB of HBM per device.

v0:
```python
import jax
import jax.numpy as jnp
from jax import lax
from jax.sharding import PartitionSpec as P

BLOCK = 128
ITERS = 3


long_range = 1.0
short_range = 0.35
nugget = 1.0
tiles_per_step = 8


def wendland(distance, reach):
    scaled = distance / reach
    remain = jnp.maximum(1.0 - scaled, 0.0)
    square = remain * remain
    return square * square * (4.0 * scaled + 1.0)


def covariance_tiles(row_points, column_points):
    delta_x = row_points[:, 0, :, None] - column_points[:, 0, None, :]
    delta_y = row_points[:, 1, :, None] - column_points[:, 1, None, :]
    delta_z = row_points[:, 2, :, None] - column_points[:, 2, None, :]
    distance = jnp.sqrt(delta_x * delta_x + delta_y * delta_y + delta_z * delta_z)
    kernel = wendland(distance, long_range) + wendland(distance, short_range)
    return row_points[:, 3, :, None] * kernel * column_points[:, 3, None, :]


def as_blocks(points):
    return points.reshape(4, -1, BLOCK).transpose(1, 0, 2)


def per_device(point_data, right_side, pair_list):
    col_devices = lax.axis_size("col")
    my_row = lax.axis_index("row")
    my_column = lax.axis_index("col")
    points = point_data.shape[1]
    blocks_here = points // BLOCK
    realizations = right_side.shape[0]
    own_blocks = as_blocks(point_data)
    row_blocks = as_blocks(lax.all_gather(point_data, "col", axis=1, tiled=True))
    column_blocks = as_blocks(lax.all_gather(point_data, "row", axis=1, tiled=True))
    row_count = row_blocks.shape[0]
    column_count = column_blocks.shape[0]
    lower_block = pair_list[0]
    upper_block = pair_list[1]
    this_device = my_row * col_devices + my_column
    device_of = (
        lower_block // blocks_here // col_devices * col_devices
        + upper_block // blocks_here % col_devices
    )
    roster_first_pair = jnp.sum((device_of < this_device).astype(jnp.int32))
    roster_pair_count = jnp.sum((device_of == this_device).astype(jnp.int32))
    roster_row_slot = jnp.clip(lower_block - my_row * col_devices * blocks_here, 0, row_count - 1)
    roster_column_slot = jnp.clip(
        upper_block // blocks_here // col_devices * blocks_here + upper_block % blocks_here,
        0,
        column_count - 1,
    )
    roster_step_count = (roster_pair_count + tiles_per_step - 1) // tiles_per_step
    plan = (
        roster_first_pair,
        roster_pair_count,
        roster_row_slot,
        roster_column_slot,
        roster_step_count,
        lower_block.shape[0],
    )
    first_pair, pair_count, row_slot, column_slot, step_count, listed = plan
    own_tiles = covariance_tiles(own_blocks, own_blocks).astype(jnp.bfloat16)

    def pick_tiles(step):
        offsets = step * tiles_per_step + jnp.arange(tiles_per_step)
        usable = offsets < pair_count
        picked = jnp.minimum(first_pair + offsets, listed - 1)
        row_pick = row_slot[picked]
        column_pick = column_slot[picked]
        tiles_now = covariance_tiles(row_blocks[row_pick], column_blocks[column_pick])
        tiles_now = jnp.where(usable[:, None, None], tiles_now, 0.0).astype(jnp.bfloat16)
        return (tiles_now, row_pick, column_pick)

    def inner(operands):
        stacked = jnp.stack(
            [jnp.sum(one_side * other_side, axis=1) for one_side, other_side in operands]
        )
        return lax.psum(stacked, ("row", "col"))

    solution = jnp.zeros_like(right_side)
    residual = right_side
    direction = right_side
    norm_now = inner(((residual, residual),))[0]
    for step in range(ITERS):
        rounded = direction.astype(jnp.bfloat16)
        product_row_direction = lax.all_gather(rounded, "col", axis=1, tiled=True)
        product_column_direction = lax.all_gather(rounded, "row", axis=1, tiled=True)
        row_direction = product_row_direction
        column_direction = product_column_direction
        row_direction = row_direction.reshape(realizations, row_count, BLOCK)
        column_direction = column_direction.reshape(realizations, column_count, BLOCK)

        def add_step(step, totals):
            into_rows, into_columns = totals
            tiles_now, row_pick, column_pick = pick_tiles(step)
            to_rows = jnp.einsum(
                "tij,ctj->cti",
                tiles_now,
                column_direction[:, column_pick],
                preferred_element_type=jnp.float32,
            )
            to_columns = jnp.einsum(
                "tij,cti->ctj",
                tiles_now,
                row_direction[:, row_pick],
                preferred_element_type=jnp.float32,
            )
            return (
                into_rows.at[:, row_pick].add(to_rows),
                into_columns.at[:, column_pick].add(to_columns),
            )

        empty_rows = jnp.zeros((realizations, row_count, BLOCK), jnp.float32)
        empty_columns = jnp.zeros((realizations, column_count, BLOCK), jnp.float32)
        into_rows, into_columns = lax.fori_loop(
            0, step_count, add_step, (empty_rows, empty_columns)
        )
        product_into_rows = into_rows.reshape(realizations, -1)
        product_into_columns = into_columns.reshape(realizations, -1)
        from_rows = lax.psum_scatter(product_into_rows, "col", scatter_dimension=1, tiled=True)
        from_columns = lax.psum_scatter(
            product_into_columns.astype(jnp.bfloat16), "row", scatter_dimension=1, tiled=True
        ).astype(jnp.float32)
        diagonal = jnp.einsum(
            "tij,ctj->cti",
            own_tiles,
            rounded.reshape(realizations, blocks_here, BLOCK),
            preferred_element_type=jnp.float32,
        )
        image = (
            nugget * direction + diagonal.reshape(realizations, points) + from_rows + from_columns
        )
        alpha = norm_now / inner(((direction, image),))[0]
        solution = solution + alpha[:, None] * direction
        residual = residual - alpha[:, None] * image
        if step + 1 < ITERS:
            norm_next = inner(((residual, residual),))[0]
            direction = residual + (norm_next / norm_now)[:, None] * direction
            norm_now = norm_next
    return (solution, residual)


def solution(mesh):
    placed = (P(None, ("row", "col")), P(None, ("row", "col")), P())
    return jax.shard_map(
        per_device,
        mesh=mesh,
        in_specs=placed,
        out_specs=(P(None, ("row", "col")), P(None, ("row", "col"))),
        check_vma=False,
    )
```

profile of v0, /device:TPU:1, one launch (start us, length us, event | category | flops | bytes accessed | tf_op | source)
XLA Modules:
  0.0 1204.8 jit_solution(9535663260100663751)
XLA Ops:
  11.2 22.7 %all_gather.26 = f32[4,2048]{1,0:T(4,128)S(1)} all-gather(f32[4,256]{1,0:T(4,128)} %param.9), channel_id=1, replica_groups=mesh['row'=8,'col'=32] {'row'}, dimensions={1}, use_global_device_ids=true | all-gather | bytes 36864 | tf_op jit(solution)/shard_map/all_gather | solution.py:45
  33.9 34.0 %all_gather.25 = f32[4,8192]{1,0:T(4,128)} all-gather(f32[4,256]{1,0:T(4,128)} %param.9), channel_id=1, replica_groups=mesh['row'=8,'col'=32] {'col'}, dimensions={1}, use_global_device_ids=true | all-gather | bytes 135168 | tf_op jit(solution)/shard_map/all_gather | solution.py:44
  67.9 18.8 %all_gather.24 = bf16[64,2048]{1,0:T(8,128)(2,1)S(1)} all-gather(bf16[64,256]{1,0:T(8,128)(2,1)} %convert_element_type.64), channel_id=1, replica_groups=mesh['row'=8,'col'=32] {'row'}, dimensions={1}, use_global_device_ids=true | all-gather | bytes 294912 | tf_op jit(solution)/shard_map/all_gather | solution.py:98
  86.8 2.6 copy_bitcast_fusion.5
  89.7 47.4 %while.42 = (s32[]{:T(128)}, f32[64,64,128]{2,0,1:T(8,128)S(1)}, f32[64,16,128]{2,0,1:T(8,128)S(1)}, s32[]{:T(128)}, s32[]{:T(128)}, /*index=5*/s32[4444]{0:T(10...) while((s32[]{:T(128)}, f32[64,64,128]{2,0,1:T(8,128)S(1)}, ...), condition=%wide.region_7.8_spmd, body=%wide.region_4.7_spmd.sunk | while | flops 41028720 | bytes 3093305 | solution.py:126
  97.4 1.8 gather_fusion.5
  109.2 1.8 gather_fusion.5
  121.1 1.8 gather_fusion.5
  133.0 1.8 gather_fusion.5
  137.9 1.5 copy_bitcast_fusion.2
  140.6 55.3 %reduce-scatter.9.cloned.1.call-done = bf16[64,256]{1,0:T(8,128)(2,1)} async-done(((bf16[64,2048]{1,0:T(8,128)(2,1)}), bf16[64,256]{1,0:T(8,128)(2,1)}) %reduce-scatter.9.cloned.1.call-update) | async-done | bytes 32784 | tf_op jit(solution)/shard_map/reduce_scatter | solution.py:132
  195.9 93.4 %reduce-scatter.7.cloned.1.call-done = f32[64,256]{1,0:T(8,128)} async-done(((f32[64,8192]{1,0:T(8,128)}), f32[64,256]{1,0:T(8,128)}) %reduce-scatter.7.cloned.1.call-update) | async-done | bytes 65552 | tf_op jit(solution)/shard_map/reduce_scatter | solution.py:131
  290.3 77.2 %all-reduce = (f32[1,64]{1,0:T(1,128)S(1)}, f32[1,64]{1,0:T(1,128)S(1)}) all-reduce(f32[1,64]{1,0:T(1,128)S(1)} %bitcast.368, f32[1,64]{1,0:T(1,128)S(1)} %bitcast.367), channel_id=1, replica_groups=mesh['row'=8,'col'=32] {'row','col'}, use_global_device_ids=true, to_apply=%region_1.2 | all-reduce | flops 128 | bytes 1024 | tf_op jit(solution)/shard_map/psum | solution.py:89
  368.6 73.4 %psum.44 = f32[1,64]{1,0:T(1,128)S(1)} all-reduce(f32[1,64]{1,0:T(1,128)S(1)} %bitcast.366), channel_id=1, replica_groups=mesh['row'=8,'col'=32] {'row','col'}, use_global_device_ids=true, to_apply=%region_13.14 | all-reduce | flops 64 | bytes 512 | tf_op jit(solution)/shard_map/psum | solution.py:89
  442.8 19.0 %all_gather.28 = bf16[64,2048]{1,0:T(8,128)(2,1)S(1)} all-gather(bf16[64,256]{1,0:T(8,128)(2,1)} %get-tuple-element.609), channel_id=1, replica_groups=mesh['row'=8,'col'=32] {'row'}, dimensions={1}, use_global_device_ids=true | all-gather | bytes 294912 | tf_op jit(solution)/shard_map/all_gather | solution.py:98
  461.8 25.4 %all-gather.6.cloned.1.call-done = bf16[64,8192]{1,0:T(8,128)(2,1)} async-done(((bf16[64,256]{1,0:T(8,128)(2,1)}), bf16[64,8192]{1,0:T(8,128)(2,1)}) %all-gather.6.cloned.1.call-update) | async-done | bytes 1048592 | tf_op jit(solution)/shard_map/all_gather | solution.py:97
  487.2 2.5 copy_bitcast_fusion.4
  490.1 47.4 %while.43 = (s32[]{:T(128)}, f32[64,64,128]{2,0,1:T(8,128)S(1)}, f32[64,16,128]{2,0,1:T(8,128)S(1)}, s32[]{:T(128)}, s32[]{:T(128)}, /*index=5*/s32[4444]{0:T(10...) while((s32[]{:T(128)}, f32[64,64,128]{2,0,1:T(8,128)S(1)}, ...), condition=%wide.region_17.18_spmd, body=%wide.region_14.17_spmd.sunk | while | flops 41028720 | bytes 3093305 | solution.py:126
  497.8 1.8 gather_fusion.11
  509.6 1.8 gather_fusion.11
  521.5 1.8 gather_fusion.11
  533.4 1.8 gather_fusion.11
  538.3 1.5 copy_bitcast_fusion.1
  540.9 55.8 %reduce-scatter.13.cloned.1.call-done = bf16[64,256]{1,0:T(8,128)(2,1)} async-done(((bf16[64,2048]{1,0:T(8,128)(2,1)}), bf16[64,256]{1,0:T(8,128)(2,1)}) %reduce-scatter.13.cloned.1.call-update) | async-done | bytes 32784 | tf_op jit(solution)/shard_map/reduce_scatter | solution.py:132
  596.8 92.5 %reduce-scatter.11.cloned.1.call-done = f32[64,256]{1,0:T(8,128)} async-done(((f32[64,8192]{1,0:T(8,128)}), f32[64,256]{1,0:T(8,128)}) %reduce-scatter.11.cloned.1.call-update) | async-done | bytes 65552 | tf_op jit(solution)/shard_map/reduce_scatter | solution.py:131
  690.2 77.3 %psum.45 = f32[1,64]{1,0:T(1,128)S(1)} all-reduce(f32[1,64]{1,0:T(1,128)S(1)} %bitcast.369), channel_id=1, replica_groups=mesh['row'=8,'col'=32] {'row','col'}, use_global_device_ids=true, to_apply=%region_21.22 | all-reduce | flops 64 | bytes 512 | tf_op jit(solution)/shard_map/psum | solution.py:89
  768.5 73.3 %psum.46 = f32[1,64]{1,0:T(1,128)S(1)} all-reduce(f32[1,64]{1,0:T(1,128)S(1)} %bitcast.365), channel_id=1, replica_groups=mesh['row'=8,'col'=32] {'row','col'}, use_global_device_ids=true, to_apply=%region_23.24 | all-reduce | flops 64 | bytes 512 | tf_op jit(solution)/shard_map/psum | solution.py:89
  843.2 19.1 %all_gather.30 = bf16[64,2048]{1,0:T(8,128)(2,1)S(1)} all-gather(bf16[64,256]{1,0:T(8,128)(2,1)} %fusion.91), channel_id=1, replica_groups=mesh['row'=8,'col'=32] {'row'}, dimensions={1}, use_global_device_ids=true | all-gather | bytes 294912 | tf_op jit(solution)/shard_map/all_gather | solution.py:98
  862.3 25.4 %all-gather.8.cloned.1.call-done = bf16[64,8192]{1,0:T(8,128)(2,1)} async-done(((bf16[64,256]{1,0:T(8,128)(2,1)}), bf16[64,8192]{1,0:T(8,128)(2,1)}) %all-gather.8.cloned.1.call-update) | async-done | bytes 1048592 | tf_op jit(solution)/shard_map/all_gather | solution.py:97
  887.7 2.5 copy_bitcast_fusion.3
  890.5 63.5 %while.44 = (s32[]{:T(128)}, f32[64,64,128]{2,0,1:T(8,128)S(1)}, f32[64,16,128]{2,0,1:T(8,128)S(1)}, s32[]{:T(128)}, s32[]{:T(128)}, /*index=5*/s32[4444]{0:T(10...) while((s32[]{:T(128)}, f32[64,64,128]{2,0,1:T(8,128)S(1)}, ...), condition=%wide.region_27.28_spmd, body=%wide.region_24.27_spmd.sunk | while | flops 41028720 | bytes 3093677 | solution.py:126
  898.4 2.1 fusion.162
  901.5 1.8 gather_fusion.17
  903.3 2.2 fusion.163
  914.2 2.1 fusion.162
  917.4 1.8 gather_fusion.17
  919.2 2.2 fusion.163
  930.0 2.1 fusion.162
  933.2 1.8 gather_fusion.17
  935.0 2.2 fusion.163
  945.9 2.1 fusion.162
  949.1 1.8 gather_fusion.17
  950.9 2.2 fusion.163
  954.9 1.5 copy_bitcast_fusion
  957.5 67.5 %reduce-scatter.17.cloned.1.call-done = bf16[64,256]{1,0:T(8,128)(2,1)} async-done(((bf16[64,2048]{1,0:T(8,128)(2,1)}), bf16[64,256]{1,0:T(8,128)(2,1)}) %reduce-scatter.17.cloned.1.call-update) | async-done | bytes 32784 | tf_op jit(solution)/shard_map/reduce_scatter | solution.py:132
  1025.0 93.4 %reduce-scatter.15.cloned.1.call-done = f32[64,256]{1,0:T(8,128)} async-done(((f32[64,8192]{1,0:T(8,128)}), f32[64,256]{1,0:T(8,128)}) %reduce-scatter.15.cloned.1.call-update) | async-done | bytes 65552 | tf_op jit(solution)/shard_map/reduce_scatter | solution.py:131
  1119.5 77.2 %psum.47 = f32[1,64]{1,0:T(1,128)S(1)} all-reduce(f32[1,64]{1,0:T(1,128)S(1)} %bitcast.370), channel_id=1, replica_groups=mesh['row'=8,'col'=32] {'row','col'}, use_global_device_ids=true, to_apply=%region_31.32 | all-reduce | flops 64 | bytes 512 | tf_op jit(solution)/shard_map/psum | solution.py:89
  1196.7 1.6 multiply_subtract_fusion
  (328 shorter events, 135.4 us)
Async XLA Ops:
  7.2 79.6 %all-gather.4.cloned.1.call-start = ((), (), s32[]{:S(2)}) async-start(), calls=%async_computation.6 | async-start | bytes 1081344 | tf_op jit(solution)/shard_map/all_gather | solution.py:97
  8.7 187.2 %reduce-scatter.9.cloned.1.call-start = ((), (), s32[]{:S(2)}) async-start(), calls=%async_computation.8 | async-start | bytes 294912 | tf_op jit(solution)/shard_map/reduce_scatter | solution.py:132
  137.9 151.5 %reduce-scatter.7.cloned.1.call-start = ((), (), s32[]{:S(2)}) async-start(), calls=%async_computation.7 | async-start | bytes 2162688 | tf_op jit(solution)/shard_map/reduce_scatter | solution.py:131
  139.4 0.7 copy-start.7
  139.4 0.9 copy-start
  139.4 347.8 %all-gather.6.cloned.1.call-start = ((), (), s32[]{:S(2)}) async-start(), calls=%async_computation.9 | async-start | bytes 1081344 | tf_op jit(solution)/shard_map/all_gather | solution.py:97
  140.1 399.8 %copy-start.14 = (f32[2,128]{1,0:T(2,128)}, f32[2,128]{1,0:T(2,128)S(1)}, u32[]{:S(2)}) copy-start(f32[2,128]{1,0:T(2,128)S(1)} %get-tuple-element.642) | copy-start | bytes 3076
  140.1 399.8 %copy-start.16 = (f32[2,128]{1,0:T(2,128)}, f32[2,128]{1,0:T(2,128)S(1)}, u32[]{:S(2)}) copy-start(f32[2,128]{1,0:T(2,128)S(1)} %get-tuple-element.643) | copy-start | bytes 3076
  140.1 399.8 %copy-start.18 = (f32[2,128]{1,0:T(2,128)}, f32[2,128]{1,0:T(2,128)S(1)}, u32[]{:S(2)}) copy-start(f32[2,128]{1,0:T(2,128)S(1)} %get-tuple-element.644) | copy-start | bytes 3076
  140.1 399.8 %copy-start.20 = (f32[2,128]{1,0:T(2,128)}, f32[2,128]{1,0:T(2,128)S(1)}, u32[]{:S(2)}) copy-start(f32[2,128]{1,0:T(2,128)S(1)} %get-tuple-element.645) | copy-start | bytes 3076
  367.5 1.1 copy-start.10
  368.6 118.6 %copy-start.1 = (f32[64,256]{1,0:T(8,128)}, f32[64,256]{1,0:T(8,128)S(1)}, u32[]{:S(2)}) copy-start(f32[64,256]{1,0:T(8,128)S(1)} %get-tuple-element.612) | copy-start | bytes 196612
  442.7 154.1 %reduce-scatter.13.cloned.1.call-start = ((), (), s32[]{:S(2)}) async-start(), calls=%async_computation.11 | async-start | bytes 294912 | tf_op jit(solution)/shard_map/reduce_scatter | solution.py:132
  538.3 151.0 %reduce-scatter.11.cloned.1.call-start = ((), (), s32[]{:S(2)}) async-start(), calls=%async_computation.10 | async-start | bytes 2162688 | tf_op jit(solution)/shard_map/reduce_scatter | solution.py:131
  539.8 0.8 copy-start.4
  539.8 227.7 %copy-start.2 = (f32[64,256]{1,0:T(8,128)S(1)}, f32[64,256]{1,0:T(8,128)}, u32[]{:S(2)}) copy-start(f32[64,256]{1,0:T(8,128)} %copy-done.1) | copy-start | bytes 196612
  539.8 347.9 %all-gather.8.cloned.1.call-start = ((), (), s32[]{:S(2)}) async-start(), calls=%async_computation.12 | async-start | bytes 1081344 | tf_op jit(solution)/shard_map/all_gather | solution.py:97
  767.5 120.2 %copy-start.12 = (f32[64]{0:T(128)}, f32[64]{0:T(128)S(1)}, u32[]{:S(2)}) copy-start(f32[64]{0:T(128)S(1)} %divide_bitcast_fusion.2) | copy-start | bytes 772
  841.8 45.9 %copy-start.22 = (f32[1,64]{1,0:T(1,128)}, f32[1,64]{1,0:T(1,128)S(1)}, u32[]{:S(2)}) copy-start(f32[1,64]{1,0:T(1,128)S(1)} %psum.46) | copy-start | bytes 772
  841.8 0.6 copy-start.8
  843.1 181.9 %reduce-scatter.17.cloned.1.call-start = ((), (), s32[]{:S(2)}) async-start(), calls=%async_computation.14 | async-start | bytes 294912 | tf_op jit(solution)/shard_map/reduce_scatter | solution.py:132
  892.1 0.5 copy-start.5
  894.4 0.6 copy-start.6
  898.4 2.2 copy-start.24
  907.9 0.5 copy-start.5
  910.3 0.6 copy-start.6
  914.2 2.2 copy-start.24
  923.7 0.5 copy-start.5
  926.1 0.6 copy-start.6
  930.0 2.2 copy-start.24
  939.6 0.5 copy-start.5
  941.9 0.6 copy-start.6
  945.9 2.2 copy-start.24
  954.9 163.6 %reduce-scatter.15.cloned.1.call-start = ((), (), s32[]{:S(2)}) async-start(), calls=%async_computation.13 | async-start | bytes 2162688 | tf_op jit(solution)/shard_map/reduce_scatter | solution.py:131
  956.4 0.8 copy-start.3
  956.4 0.8 copy-start.15
  956.4 0.8 copy-start.17
  956.4 0.8 copy-start.19
  956.4 0.8 copy-start.21
  956.4 162.0 %copy-start.9 = (f32[64]{0:T(128)S(1)}, f32[64]{0:T(128)}, u32[]{:S(2)}) copy-start(f32[64]{0:T(128)} %copy-done.8) | copy-start | bytes 772
  956.4 240.2 %copy-start.23 = (f32[1,64]{1,0:T(1,128)S(1)}, f32[1,64]{1,0:T(1,128)}, u32[]{:S(2)}) copy-start(f32[1,64]{1,0:T(1,128)} %copy-done.22) | copy-start | bytes 772
  956.4 240.2 %copy-start.11 = (f32[64]{0:T(128)S(1)}, f32[64]{0:T(128)}, u32[]{:S(2)}) copy-start(f32[64]{0:T(128)} %copy-done.10) | copy-start | bytes 772
  956.4 240.2 %copy-start.13 = (f32[64]{0:T(128)S(1)}, f32[64]{0:T(128)}, u32[]{:S(2)}) copy-start(f32[64]{0:T(128)} %copy-done.12) | copy-start | bytes 772
Sparse Core Ops, SparseCore 0:
  11.0 52.1 all-gather.3
  138.0 57.8 reduce-scatter.8
  200.3 89.0 reduce-scatter.6
  442.8 44.3 all-gather.5
  538.4 58.3 reduce-scatter.12
  600.4 88.7 reduce-scatter.10
  843.3 44.3 all-gather.7
  955.0 69.9 reduce-scatter.16
  1029.3 89.0 reduce-scatter.14
where the time goes:
time: 1210 us; the launch traced here: 1200 us
  waiting for transfers between devices  509 us (42%)
  blocking collectives  492 us (41%)
  local copies, waits for them, and re-layouts  94.4 us (8%)
  other arithmetic  52 us (4%)
  matrix products  40.9 us (3%)
  between operations  14.9 us (1%)
    psum x5, blocking collectives, inner(): return lax.psum(stacked, ('row', 'col'))  378 us
    reduce_scatter x3, waiting for transfers between devices, per_device(): lax.psum_scatter(product_into_rows, 'col', scatter_dimension=1, tiled=True)  279 us
    reduce_scatter x3, waiting for transfers between devices, per_device(): lax.psum_scatter(product_into_columns.astype(jnp.bfloat16), 'row', scatte...  179 us
    all_gather x3, blocking collectives, per_device(): lax.all_gather(rounded, 'row', axis=1, tiled=True)  56.9 us
    all_gather x3, waiting for transfers between devices, per_device(): product_row_direction = lax.all_gather(rounded, 'col', axis=1, tiled=True)  50.8 us
    all_gather x1, blocking collectives, per_device(): lax.all_gather(point_data, 'col', axis=1, tiled=True)  34 us
  transfers between devices with their start and end apart: 9, of which 8 were waited for; matrix products, arithmetic and copies ran while one was open for 1% of the time, Pallas kernels for 0%

commit v1 on v0

v1 whole, which is shorter than its diff:
```python
import functools

import jax
import jax.numpy as jnp
from jax import lax
from jax.experimental import pallas as pl
from jax.experimental.pallas import tpu as pltpu
from jax.sharding import PartitionSpec as P

SIDE = 4
BLOCK = 128
MESH = pl.DeviceIdType.MESH
long_range = 1.0
short_range = 0.35
nugget = 1.0
PHASES = 26


def covariance(xj, yj, zj, sj, xi, yi, zi, si):
    dx, dy, dz = xj - xi, yj - yi, zj - zi
    d = jnp.sqrt(dx * dx + dy * dy + dz * dz)

    def wendland(u):
        remain = jnp.maximum(1.0 - u, 0.0)
        square = remain * remain
        return square * square * (4.0 * u + 1.0)

    return sj * (wendland(d * (1.0 / long_range)) + wendland(d * (1.0 / short_range))) * si


def kernel(side, depth, point_ref, right_ref, solution_ref, residual_ref,
           g_pts, g_vec0, g_vec1, g_vec2, g_vec3, line_pts, zs_pts, zr_pts, zs_vec, zr_vec, h_pts, h_vec,
           tiles, p_all, r_all, ar_one, ar_two, table_v, table_s, coef, send, recv, local_sem):
    g_vec = (g_vec0, g_vec1, g_vec2, g_vec3)
    chips = side * side
    slots = 4 * chips
    zslots = 2 * depth
    R = right_ref.shape[0]
    my_z = lax.axis_index("row")
    my_col = lax.axis_index("col")
    core = my_col % 2
    chip = my_col // 2
    xx = chip % side
    yy = chip // side
    zs = my_z * 2 + core
    own = (core * chips + chip) * 2

    def device(zslot, chip_):
        return (zslot // 2, chip_ * 2 + zslot % 2)

    def shifted(ox, oy):
        return ((yy + oy) % side) * side + (xx + ox) % side

    def plane_peer(o):
        return device(zs, shifted(o % side, o // side))

    def line_peer(o):
        return device((my_z + o) % depth * 2 + core, chip)

    def pillar_peer(o):
        return device((zs + o) % zslots, chip)

    def neighbour(n, oz):
        return device((zs + oz + zslots) % zslots, shifted(n // 3 - 1 + side, n % 3 - 1 + side))

    def push(src, dst, phase, peer):
        pltpu.make_async_remote_copy(
            src_ref=src, dst_ref=dst, send_sem=send.at[phase], recv_sem=recv.at[phase],
            device_id=peer, device_id_type=MESH,
        ).start()

    phases = []

    def new_phase(view):
        phases.append(view)
        return len(phases) - 1

    def arrived(phase):
        view = phases[phase]
        pltpu.make_async_copy(view, view, recv.at[phase]).wait()

    def loop(lo, hi, body):
        lax.fori_loop(lo, hi, lambda i, c: (body(i), c)[1], 0)

    def plane_start(buf):
        phase = new_phase(buf.at[pl.ds(0, 2 * (chips - 1))])
        part = buf.at[pl.ds(own, 2)]
        loop(1, chips, lambda o: push(part, part, phase, plane_peer(o)))
        return phase

    def forward_start(buf):
        phase = new_phase(buf.at[pl.ds(0, 2 * chips)])
        part = buf.at[pl.ds(core * 2 * chips, 2 * chips)]
        push(part, part, phase, device(my_z * 2 + 1 - core, chip))
        return phase

    def column_start(buf, staged, into, table):
        phase = new_phase(into.at[pl.ds(0, 2 * (depth - 1))])

        def select(t):
            staged[t] = buf[table_s[table, 4, t]]

        loop(0, 2 * depth, select)
        into[2 * my_z] = staged[2 * my_z]
        into[2 * my_z + 1] = staged[2 * my_z + 1]

        def one(o):
            z_to = (my_z + o) % depth
            push(staged.at[pl.ds(2 * z_to, 2)], into.at[pl.ds(2 * my_z, 2)], phase, line_peer(o))

        loop(1, depth, one)
        return phase

    def column_sum(into):
        pair = []
        for half in range(2):
            total = into[half].astype(jnp.float32)
            for z in range(1, depth):
                total = total + into[2 * z + half].astype(jnp.float32)
            pair.append(total)
        return pair

    def halo_start(buf):
        phase = new_phase(buf.at[pl.ds(0, 34)])

        def one(n):
            there = (8 - n) * 4

            @pl.when(n != 4)
            def _():
                push(buf.at[pl.ds(17, 2)], buf.at[pl.ds(there + 1, 2)], phase, neighbour(n, 0))

            push(buf.at[pl.ds(18, 1)], buf.at[pl.ds(there, 1)], phase, neighbour(n, 1))
            push(buf.at[pl.ds(17, 1)], buf.at[pl.ds(there + 3, 1)], phase, neighbour(n, -1))

        loop(0, 9, one)
        return phase

    pts = point_ref[...]
    for half in range(2):
        here = pts[:, half * BLOCK:(half + 1) * BLOCK]
        low = jnp.broadcast_to(jnp.floor(jnp.min(here, axis=1, keepdims=True)), (4, BLOCK))
        cx = jnp.clip(low[0:1], 0.0, side - 1.0)
        cy = jnp.clip(low[1:2], 0.0, side - 1.0)
        cz = jnp.clip(low[2:3], 0.0, 4.0 * depth - 1.0)
        slab = jnp.floor(cz * 0.25)
        level = cz - 4.0 * slab
        upper = jnp.floor(level * 0.5)
        slot = (upper * chips + cy * side + cx) * 2.0 + (level - 2.0 * upper)
        g_pts[own + half] = jnp.zeros((8, BLOCK), jnp.float32)
        g_pts[own + half, 0:4, :] = here
        g_pts[own + half, 4:5, :] = slab * slots + slot
        g_pts[own + half, 5:6, :] = slot
        g_pts[own + half, 6:7, :] = slab
        g_vec[0][own + half] = right_ref[:, half * BLOCK:(half + 1) * BLOCK].astype(jnp.bfloat16)
        line_pts[2 * my_z + half] = g_pts[own + half]
    g_pts[slots] = jnp.zeros((8, BLOCK), jnp.float32)
    for v in range(4):
        g_vec[v][slots] = jnp.zeros((R, BLOCK), jnp.bfloat16)

    barrier = pltpu.get_barrier_semaphore()

    def greet(peer):
        pl.semaphore_signal(barrier, inc=1, device_id=peer, device_id_type=MESH)

    loop(1, chips, lambda o: greet(plane_peer(o)))
    loop(1, zslots, lambda o: greet(pillar_peer(o)))

    def greet_three(n):
        @pl.when(n != 4)
        def _():
            greet(neighbour(n, 0))

        greet(neighbour(n, 1))
        greet(neighbour(n, -1))

    loop(0, 9, greet_three)
    pl.semaphore_wait(barrier, chips - 1 + zslots - 1 + 26)

    pts_plane = plane_start(g_pts)
    line = new_phase(line_pts.at[pl.ds(0, 2 * (depth - 1))])
    mine = line_pts.at[pl.ds(2 * my_z, 2)]
    loop(1, depth, lambda o: push(mine, mine, line, line_peer(o)))
    b_plane = plane_start(g_vec[0])
    arrived(pts_plane)
    pts_forward = forward_start(g_pts)
    arrived(line)
    arrived(pts_forward)

    lane = lax.broadcasted_iota(jnp.int32, (8, BLOCK), 1)
    target = ((lane // 2) * slots + (own + lane % 2)).astype(jnp.float32)
    gap = jnp.float32(slots)

    def find(k, acc):
        return jnp.minimum(acc, jnp.where(g_pts[k] == target, lax.convert_element_type(k, jnp.float32), gap))

    into_cells = lax.fori_loop(0, slots, find, jnp.full((8, BLOCK), gap, jnp.float32))
    table_v[0] = jnp.clip(into_cells.astype(jnp.int32), 0, slots)
    slab_here = lax.convert_element_type(my_z, jnp.float32)

    def place(t, acc):
        tile = line_pts[t]
        value = jnp.where(tile[6:7] == slab_here, tile[5:6], gap)
        return jnp.where(lane == t, jnp.broadcast_to(value, (8, BLOCK)), acc)

    into_homes = lax.fori_loop(0, 2 * depth, place, jnp.full((8, BLOCK), gap, jnp.float32))
    table_v[1] = jnp.clip(into_homes.astype(jnp.int32), 0, slots)
    copy = pltpu.make_async_copy(table_v, table_s, local_sem)
    copy.start()
    copy.wait()

    pts_column = column_start(g_pts, zs_pts, zr_pts, 0)
    arrived(b_plane)
    b_forward = forward_start(g_vec[0])
    arrived(pts_column)
    for half, total in enumerate(column_sum(zr_pts)):
        h_pts[17 + half] = total
    pts_halo = halo_start(h_pts)
    arrived(b_forward)
    b_column = column_start(g_vec[0], zs_vec.at[0], zr_vec.at[0], 0)
    arrived(pts_halo)

    def tile_column(n):
        for level in range(4):
            other = jnp.transpose(h_pts[n * 4 + level])
            xj, yj, zj, sj = (other[:, a:a + 1] for a in range(4))
            for half in range(2):
                rows, lanes = pl.ds(level * BLOCK, BLOCK), pl.ds(half * BLOCK, BLOCK)
                if not 0 <= level - half <= 2:
                    tiles[n, rows, lanes] = jnp.zeros((BLOCK, BLOCK), jnp.bfloat16)
                    continue
                xi, yi, zi, si = (h_pts[17 + half, a:a + 1, :] for a in range(4))
                tiles[n, rows, lanes] = covariance(xj, yj, zj, sj, xi, yi, zi, si).astype(jnp.bfloat16)

    loop(0, 9, tile_column)

    arrived(b_column)
    for half, total in enumerate(column_sum(zr_vec.at[0])):
        h_vec[0, 17 + half] = total.astype(jnp.bfloat16)
    halo = halo_start(h_vec.at[0])

    eye = lax.broadcasted_iota(jnp.int32, (R, BLOCK), 0) == lax.broadcasted_iota(jnp.int32, (R, BLOCK), 1)
    row8 = lax.broadcasted_iota(jnp.int32, (8, BLOCK), 0)

    def as_lanes(a, b):
        total = jnp.sum(a * b, axis=1, keepdims=True)
        return jnp.sum(jnp.where(eye, total, 0.0), axis=0, keepdims=True)

    def as_rows(values):
        column = jnp.sum(jnp.where(eye, values, 0.0), axis=1, keepdims=True)
        return jnp.broadcast_to(column, (R, BLOCK))

    def sum_start(step, rows):
        tile = jnp.zeros((8, BLOCK), jnp.float32)
        for i, value in enumerate(rows):
            tile = jnp.where(row8 == i, value, tile)
        buf = ar_one.at[step]
        buf[chip] = tile
        phase = new_phase(buf.at[pl.ds(0, chips - 1)])
        part = buf.at[pl.ds(chip, 1)]
        loop(1, chips, lambda o: push(part, part, phase, plane_peer(o)))
        return phase

    def sum_second(step, phase):
        arrived(phase)
        buf, second = ar_one.at[step], ar_two.at[step]
        total = buf[0]
        for i in range(1, chips):
            total = total + buf[i]
        second[zs] = total
        phase = new_phase(second.at[pl.ds(0, zslots - 1)])
        part = second.at[pl.ds(zs, 1)]
        loop(1, zslots, lambda o: push(part, part, phase, pillar_peer(o)))
        return phase

    def sum_finish(step, phase):
        arrived(phase)
        second = ar_two.at[step]
        total = second[0]
        for i in range(1, zslots):
            total = total + second[i]
        return total

    planes, forwards, columns = {}, {}, {}
    norm_now = None
    for step in range(3):
        arrived(halo)

        def column(n, acc, step=step):
            parts = []
            for level in range(4):
                k = n * 4 + level
                if step == 0:
                    parts.append(h_vec[0, k])
                    continue
                if step == 1:
                    p_old = h_vec[0, k].astype(jnp.float32)
                    r_old = p_old
                else:
                    p_old, r_old = p_all[k], r_all[k]
                image = nugget * p_old + h_vec[step, k].astype(jnp.float32)
                r_new = r_old - coef[2 * step - 2] * image
                p_new = r_new + coef[2 * step - 1] * p_old
                r_all[k] = r_new
                p_all[k] = p_new
                parts.append(p_new.astype(jnp.bfloat16))
            lhs = jnp.concatenate(parts, axis=1)
            return acc + jnp.dot(lhs, tiles[n], preferred_element_type=jnp.float32)

        product = lax.fori_loop(0, 9, column, jnp.zeros((R, 2 * BLOCK), jnp.float32))
        pq = rq = qq = rr = jnp.zeros((R, BLOCK), jnp.float32)
        for half in range(2):
            if step == 0:
                p_own = h_vec[0, 17 + half].astype(jnp.float32)
                r_own = p_own
            else:
                p_own, r_own = p_all[17 + half], r_all[17 + half]
            rounded = product[:, half * BLOCK:(half + 1) * BLOCK].astype(jnp.bfloat16)
            g_vec[step + 1][own + half] = rounded
            if step < 2:
                h_vec[step + 1, 17 + half] = rounded
            q = nugget * p_own + rounded.astype(jnp.float32)
            pq, rq, qq = pq + p_own * q, rq + r_own * q, qq + q * q
            rr = rr + r_own * r_own
        if step < 2:
            halo = halo_start(h_vec.at[step + 1])
        one = jnp.float32(1.0)
        rows = [as_lanes(a, one) for a in ((pq, rq, qq, rr) if step == 0 else (pq, rq, qq))]
        ar = sum_start(step, rows)
        planes[step] = plane_start(g_vec[step + 1])
        if step > 0:
            arrived(planes[step - 1])
            forwards[step - 1] = forward_start(g_vec[step])
        ar = sum_second(step, ar)
        if step > 0:
            arrived(forwards[step - 1])
            columns[step - 1] = column_start(g_vec[step], zs_vec.at[step], zr_vec.at[step], 1)
        totals = sum_finish(step, ar)
        if step == 0:
            norm_now = totals[3:4]
        alpha = norm_now / totals[0:1]
        norm_next = jnp.maximum(norm_now - 2.0 * alpha * totals[1:2] + alpha * alpha * totals[2:3], 0.0)
        coef[2 * step] = as_rows(alpha)
        coef[2 * step + 1] = as_rows(norm_next / norm_now)
        norm_now = norm_next

    arrived(planes[2])
    forwards[2] = forward_start(g_vec[3])
    arrived(forwards[2])
    columns[2] = column_start(g_vec[3], zs_vec.at[3], zr_vec.at[3], 1)
    for step in range(3):
        arrived(columns[step])
    images = [column_sum(zr_vec.at[step + 1]) for step in range(3)]
    for half in range(2):
        lanes = pl.ds(half * BLOCK, BLOCK)
        residual = direction = right_ref[:, lanes]
        total = jnp.zeros_like(residual)
        for step in range(3):
            total = total + coef[2 * step] * direction
            residual = residual - coef[2 * step] * (nugget * direction + images[step][half])
            if step < 2:
                direction = residual + coef[2 * step + 1] * direction
        solution_ref[:, lanes] = total
        residual_ref[:, lanes] = residual

    assert len(phases) == PHASES
    for phase, view in enumerate(phases):
        pltpu.make_async_copy(view, view, send.at[phase]).wait()


def per_device(side, depth, point_data, right_side, pair_list):
    R = right_side.shape[0]
    chips = side * side
    f32, bf16 = jnp.float32, jnp.bfloat16
    vmem = pl.BlockSpec(memory_space=pltpu.VMEM)
    out = jax.ShapeDtypeStruct(right_side.shape, f32)
    return pl.pallas_call(
        functools.partial(kernel, side, depth),
        out_shape=(out, out),
        in_specs=[vmem, vmem],
        out_specs=(vmem, vmem),
        scratch_shapes=[
            pltpu.VMEM((4 * chips + 1, 8, BLOCK), f32),
            *[pltpu.VMEM((4 * chips + 1, R, BLOCK), bf16)] * 4,
            pltpu.VMEM((2 * depth, 8, BLOCK), f32),
            pltpu.VMEM((2 * depth, 8, BLOCK), f32),
            pltpu.VMEM((2 * depth, 8, BLOCK), f32),
            pltpu.VMEM((4, 2 * depth, R, BLOCK), bf16),
            pltpu.VMEM((4, 2 * depth, R, BLOCK), bf16),
            pltpu.VMEM((36, 8, BLOCK), f32),
            pltpu.VMEM((3, 36, R, BLOCK), bf16),
            pltpu.VMEM((9, 4 * BLOCK, 2 * BLOCK), bf16),
            pltpu.VMEM((36, R, BLOCK), f32),
            pltpu.VMEM((36, R, BLOCK), f32),
            pltpu.VMEM((3, chips, 8, BLOCK), f32),
            pltpu.VMEM((3, 2 * depth, 8, BLOCK), f32),
            pltpu.VMEM((2, 8, BLOCK), jnp.int32),
            pltpu.SMEM((2, 8, BLOCK), jnp.int32),
            pltpu.VMEM((6, R, BLOCK), f32),
            pltpu.SemaphoreType.DMA((PHASES,)),
            pltpu.SemaphoreType.DMA((PHASES,)),
            pltpu.SemaphoreType.DMA,
        ],
        compiler_params=pltpu.CompilerParams(
            collective_id=0, has_side_effects=True, vmem_limit_bytes=40 << 20
        ),
    )(point_data, right_side)


def build(mesh, side):
    depth = mesh.shape["row"]
    placed = P(None, ("row", "col"))
    return jax.shard_map(
        functools.partial(per_device, side, depth),
        mesh=mesh,
        in_specs=(placed, placed, P()),
        out_specs=(placed, placed),
        check_vma=False,
    )


def solution(mesh):
    return build(mesh, SIDE)
```

time: 1210 us -> 110 us (0.09)
  waiting for transfers between devices: 509 us -> 0 us
  blocking collectives: 492 us -> 0 us
  Pallas kernels: 0 us -> 107 us
  local copies, waits for them, and re-layouts: 94.4 us -> 2.78 us
  other arithmetic: 52 us -> 0 us
  matrix products: 40.9 us -> 0 us
  between operations: 14.9 us -> 0.65 us
    reduce_scatter x6 -> x0, waiting for transfers between devices: 458 us -> none  [the longest x3 279 us: per_device(): lax.psum_scatter(product_into_rows, 'col', scatter_dimension=1, tiled=True)]
    psum x5 -> x0, blocking collectives: 378 us -> none  [inner(): return lax.psum(stacked, ('row', 'col'))]
    all_gather x5 -> x0, blocking collectives: 114 us -> none  [the longest x3 56.9 us: per_device(): lax.all_gather(rounded, 'row', axis=1, tiled=True)]
    pallas_call x0 -> x1, Pallas kernels: none -> 107 us  [per_device(): pl.pallas_call(functools.partial(kernel, side, depth), out_shape=(out, ou...]
    gather x72 -> x0, local copies, waits for them, and re-layouts: 68.3 us -> none  [the longest x12 21.6 us: add_step(): row_direction[:, row_pick]]
    all_gather x3 -> x0, waiting for transfers between devices: 50.8 us -> none  [per_device(): product_row_direction = lax.all_gather(rounded, 'col', axis=1, tiled=True)]
    dot_general x27 -> x0, matrix products: 40.9 us -> none  [the longest x12 20 us: add_step(): jnp.einsum('tij,cti->ctj', tiles_now, row_direction[:, row_pick], preferr...]
    scatter-add x24 -> x0, other arithmetic: 22.4 us -> none  [the longest x12 11.2 us: add_step(): into_rows.at[:, row_pick].add(to_rows)]
  transfers between devices with their start and end apart: 9 -> 0, of which waited for: 8 -> 0; matrix products, arithmetic and copies ran while one was open for 1% -> 0% of each run, Pallas kernels for 0% -> 0%
where the time goes in v1:
time: 110 us
  Pallas kernels  107 us (97%)
  local copies, waits for them, and re-layouts  2.78 us (3%)
    pallas_call x1, Pallas kernels, per_device(): pl.pallas_call(functools.partial(kernel, side, depth), out_shape=(out, ou...  107 us
    unnamed x6, local copies, waits for them, and re-layouts  2.78 us

profile of v1, /device:TPU:1, one launch (start us, length us, event | category | flops | bytes accessed | tf_op | source)
XLA Modules:
  0.0 110.1 jit_solution(3378695082053590690)
XLA Ops:
  0.6 0.0 copy-start
  0.6 0.8 copy-done
  1.5 0.0 copy-start.1
  1.5 0.7 copy-done.1
  2.2 106.6 %shard_map.41 = (f32[64,256]{1,0:T(8,128)S(1)}, f32[64,256]{1,0:T(8,128)S(1)}) custom-call(f32[4,256]{1,0:T(4,128)S(1)} %copy-done.1, f32[64,256]{1,0:T(8,128)S(1)} %copy-done), custom_call_target="tpu_custom_call" | custom-call | tf_op jit(solution)/shard_map/pallas_call | solution.py:377
  108.8 0.6 copy.6
  109.4 0.6 copy.7
Async XLA Ops:
  0.6 0.8 copy-start
  1.5 0.7 copy-start.1

commit v2 on v1

--- a/solution.py
+++ b/solution.py
@@ -13,7 +13,8 @@
 long_range = 1.0
 short_range = 0.35
 nugget = 1.0
-PHASES = 26
+CHUNKS = (4, 1, 1, 4)
+PHASES = 14 + 3 * sum(CHUNKS)
 
 
 def covariance(xj, yj, zj, sj, xi, yi, zi, si):
@@ -28,14 +29,16 @@
     return sj * (wendland(d * (1.0 / long_range)) + wendland(d * (1.0 / short_range))) * si
 
 
-def kernel(side, depth, point_ref, right_ref, solution_ref, residual_ref,
-           g_pts, g_vec0, g_vec1, g_vec2, g_vec3, line_pts, zs_pts, zr_pts, zs_vec, zr_vec, h_pts, h_vec,
-           tiles, p_all, r_all, ar_one, ar_two, table_v, table_s, coef, send, recv, local_sem):
-    g_vec = (g_vec0, g_vec1, g_vec2, g_vec3)
+def kernel(side, depth, point_ref, right_ref, solution_ref, residual_ref, *scratch):
     chips = side * side
     slots = 4 * chips
     zslots = 2 * depth
     R = right_ref.shape[0]
+    g_vec = [list(scratch[sum(CHUNKS[:v]):sum(CHUNKS[:v + 1])]) for v in range(4)]
+    zs_vec = scratch[sum(CHUNKS):sum(CHUNKS) + 4]
+    zr_vec = scratch[sum(CHUNKS) + 4:sum(CHUNKS) + 8]
+    (g_pts, line_pts, zs_pts, zr_pts, h_pts, h_vec, tiles, p_all, r_all, ar_one, ar_two,
+     table_v, table_s, coef, send, recv, local_sem) = scratch[sum(CHUNKS) + 8:]
     my_z = lax.axis_index("row")
     my_col = lax.axis_index("col")
     core = my_col % 2
@@ -44,6 +47,11 @@
     yy = chip // side
     zs = my_z * 2 + core
     own = (core * chips + chip) * 2
+    sibling = (my_z, chip * 2 + 1 - core)
+
+    def rows_of(v, ch):
+        size = R // CHUNKS[v]
+        return pl.ds(ch * size, size)
 
     def device(zslot, chip_):
         return (zslot // 2, chip_ * 2 + zslot % 2)
@@ -91,16 +99,13 @@
     def forward_start(buf):
         phase = new_phase(buf.at[pl.ds(0, 2 * chips)])
         part = buf.at[pl.ds(core * 2 * chips, 2 * chips)]
-        push(part, part, phase, device(my_z * 2 + 1 - core, chip))
+        push(part, part, phase, sibling)
         return phase
 
     def column_start(buf, staged, into, table):
         phase = new_phase(into.at[pl.ds(0, 2 * (depth - 1))])
-
-        def select(t):
+        for t in range(2 * depth):
             staged[t] = buf[table_s[table, 4, t]]
-
-        loop(0, 2 * depth, select)
         into[2 * my_z] = staged[2 * my_z]
         into[2 * my_z + 1] = staged[2 * my_z + 1]
 
@@ -135,6 +140,34 @@
 
         loop(0, 9, one)
         return phase
+
+    class Journey:
+        def __init__(self, v, table):
+            self.v, self.table, self.count = v, table, CHUNKS[v]
+            self.planes = [plane_start(buf) for buf in g_vec[v]]
+            self.forwards, self.columns = [], []
+
+        def forward(self):
+            ch = len(self.forwards)
+            arrived(self.planes[ch])
+            self.forwards.append(forward_start(g_vec[self.v][ch]))
+
+        def column(self):
+            ch = len(self.columns)
+            arrived(self.forwards[ch])
+            self.columns.append(column_start(
+                g_vec[self.v][ch], zs_vec[self.v].at[ch], zr_vec[self.v].at[ch], self.table))
+
+        def through(self):
+            self.forward()
+            for _ in range(1, self.count):
+                self.forward()
+                self.column()
+            self.column()
+
+        def sums(self, ch):
+            arrived(self.columns[ch])
+            return column_sum(zr_vec[self.v].at[ch])
 
     pts = point_ref[...]
     for half in range(2):
@@ -152,11 +185,14 @@
         g_pts[own + half, 4:5, :] = slab * slots + slot
         g_pts[own + half, 5:6, :] = slot
         g_pts[own + half, 6:7, :] = slab
-        g_vec[0][own + half] = right_ref[:, half * BLOCK:(half + 1) * BLOCK].astype(jnp.bfloat16)
         line_pts[2 * my_z + half] = g_pts[own + half]
+        for ch in range(CHUNKS[0]):
+            part = right_ref[rows_of(0, ch), half * BLOCK:(half + 1) * BLOCK]
+            g_vec[0][ch][own + half] = part.astype(jnp.bfloat16)
     g_pts[slots] = jnp.zeros((8, BLOCK), jnp.float32)
     for v in range(4):
-        g_vec[v][slots] = jnp.zeros((R, BLOCK), jnp.bfloat16)
+        for buf in g_vec[v]:
+            buf[slots] = jnp.zeros((R // CHUNKS[v], BLOCK), jnp.bfloat16)
 
     barrier = pltpu.get_barrier_semaphore()
 
@@ -164,60 +200,50 @@
         pl.semaphore_signal(barrier, inc=1, device_id=peer, device_id_type=MESH)
 
     loop(1, chips, lambda o: greet(plane_peer(o)))
-    loop(1, zslots, lambda o: greet(pillar_peer(o)))
-
-    def greet_three(n):
-        @pl.when(n != 4)
-        def _():
-            greet(neighbour(n, 0))
-
-        greet(neighbour(n, 1))
-        greet(neighbour(n, -1))
-
-    loop(0, 9, greet_three)
-    pl.semaphore_wait(barrier, chips - 1 + zslots - 1 + 26)
+    loop(1, depth, lambda o: greet(line_peer(o)))
+    greet(sibling)
+    pl.semaphore_wait(barrier, chips - 1 + depth - 1 + 1)
 
     pts_plane = plane_start(g_pts)
     line = new_phase(line_pts.at[pl.ds(0, 2 * (depth - 1))])
     mine = line_pts.at[pl.ds(2 * my_z, 2)]
     loop(1, depth, lambda o: push(mine, mine, line, line_peer(o)))
-    b_plane = plane_start(g_vec[0])
+    inward = Journey(0, 0)
     arrived(pts_plane)
     pts_forward = forward_start(g_pts)
     arrived(line)
-    arrived(pts_forward)
 
     lane = lax.broadcasted_iota(jnp.int32, (8, BLOCK), 1)
     target = ((lane // 2) * slots + (own + lane % 2)).astype(jnp.float32)
     gap = jnp.float32(slots)
-
-    def find(k, acc):
-        return jnp.minimum(acc, jnp.where(g_pts[k] == target, lax.convert_element_type(k, jnp.float32), gap))
-
-    into_cells = lax.fori_loop(0, slots, find, jnp.full((8, BLOCK), gap, jnp.float32))
-    table_v[0] = jnp.clip(into_cells.astype(jnp.int32), 0, slots)
     slab_here = lax.convert_element_type(my_z, jnp.float32)
-
-    def place(t, acc):
+    acc = jnp.full((8, BLOCK), gap, jnp.float32)
+    for t in range(2 * depth):
         tile = line_pts[t]
         value = jnp.where(tile[6:7] == slab_here, tile[5:6], gap)
-        return jnp.where(lane == t, jnp.broadcast_to(value, (8, BLOCK)), acc)
-
-    into_homes = lax.fori_loop(0, 2 * depth, place, jnp.full((8, BLOCK), gap, jnp.float32))
-    table_v[1] = jnp.clip(into_homes.astype(jnp.int32), 0, slots)
+        acc = jnp.where(lane == t, jnp.broadcast_to(value, (8, BLOCK)), acc)
+    table_v[1] = jnp.clip(acc.astype(jnp.int32), 0, slots)
+
+    arrived(pts_forward)
+    acc = jnp.full((8, BLOCK), gap, jnp.float32)
+    for k in range(slots):
+        acc = jnp.minimum(acc, jnp.where(g_pts[k] == target, jnp.float32(k), gap))
+    table_v[0] = jnp.clip(acc.astype(jnp.int32), 0, slots)
     copy = pltpu.make_async_copy(table_v, table_s, local_sem)
     copy.start()
     copy.wait()
 
     pts_column = column_start(g_pts, zs_pts, zr_pts, 0)
-    arrived(b_plane)
-    b_forward = forward_start(g_vec[0])
+    inward.through()
     arrived(pts_column)
     for half, total in enumerate(column_sum(zr_pts)):
         h_pts[17 + half] = total
     pts_halo = halo_start(h_pts)
-    arrived(b_forward)
-    b_column = column_start(g_vec[0], zs_vec.at[0], zr_vec.at[0], 0)
+    for ch in range(CHUNKS[0]):
+        for half, total in enumerate(inward.sums(ch)):
+            h_vec[0, 17 + half, rows_of(0, ch), :] = total.astype(jnp.bfloat16)
+    halo = halo_start(h_vec.at[0])
+
     arrived(pts_halo)
 
     def tile_column(n):
@@ -234,16 +260,11 @@
 
     loop(0, 9, tile_column)
 
-    arrived(b_column)
-    for half, total in enumerate(column_sum(zr_vec.at[0])):
-        h_vec[0, 17 + half] = total.astype(jnp.bfloat16)
-    halo = halo_start(h_vec.at[0])
-
     eye = lax.broadcasted_iota(jnp.int32, (R, BLOCK), 0) == lax.broadcasted_iota(jnp.int32, (R, BLOCK), 1)
     row8 = lax.broadcasted_iota(jnp.int32, (8, BLOCK), 0)
 
-    def as_lanes(a, b):
-        total = jnp.sum(a * b, axis=1, keepdims=True)
+    def as_lanes(values):
+        total = jnp.sum(values, axis=1, keepdims=True)
         return jnp.sum(jnp.where(eye, total, 0.0), axis=0, keepdims=True)
 
     def as_rows(values):
@@ -281,12 +302,12 @@
             total = total + second[i]
         return total
 
-    planes, forwards, columns = {}, {}, {}
+    outward = []
     norm_now = None
     for step in range(3):
         arrived(halo)
-
-        def column(n, acc, step=step):
+        product = jnp.zeros((R, 2 * BLOCK), jnp.float32)
+        for n in range(9):
             parts = []
             for level in range(4):
                 k = n * 4 + level
@@ -305,9 +326,7 @@
                 p_all[k] = p_new
                 parts.append(p_new.astype(jnp.bfloat16))
             lhs = jnp.concatenate(parts, axis=1)
-            return acc + jnp.dot(lhs, tiles[n], preferred_element_type=jnp.float32)
-
-        product = lax.fori_loop(0, 9, column, jnp.zeros((R, 2 * BLOCK), jnp.float32))
+            product = product + jnp.dot(lhs, tiles[n], preferred_element_type=jnp.float32)
         pq = rq = qq = rr = jnp.zeros((R, BLOCK), jnp.float32)
         for half in range(2):
             if step == 0:
@@ -316,52 +335,57 @@
             else:
                 p_own, r_own = p_all[17 + half], r_all[17 + half]
             rounded = product[:, half * BLOCK:(half + 1) * BLOCK].astype(jnp.bfloat16)
-            g_vec[step + 1][own + half] = rounded
             if step < 2:
                 h_vec[step + 1, 17 + half] = rounded
+            for ch in range(CHUNKS[step + 1]):
+                size = R // CHUNKS[step + 1]
+                g_vec[step + 1][ch][own + half] = rounded[ch * size:(ch + 1) * size]
             q = nugget * p_own + rounded.astype(jnp.float32)
             pq, rq, qq = pq + p_own * q, rq + r_own * q, qq + q * q
             rr = rr + r_own * r_own
+        rows = [as_lanes(a) for a in ((pq, rq, qq, rr) if step == 0 else (pq, rq, qq))]
+        ar = sum_start(step, rows)
         if step < 2:
             halo = halo_start(h_vec.at[step + 1])
-        one = jnp.float32(1.0)
-        rows = [as_lanes(a, one) for a in ((pq, rq, qq, rr) if step == 0 else (pq, rq, qq))]
-        ar = sum_start(step, rows)
-        planes[step] = plane_start(g_vec[step + 1])
-        if step > 0:
-            arrived(planes[step - 1])
-            forwards[step - 1] = forward_start(g_vec[step])
+        outward.append(Journey(step + 1, 1))
+        if step == 1:
+            outward[0].forward()
         ar = sum_second(step, ar)
-        if step > 0:
-            arrived(forwards[step - 1])
-            columns[step - 1] = column_start(g_vec[step], zs_vec.at[step], zr_vec.at[step], 1)
+        if step == 1:
+            outward[0].column()
+        if step == 2:
+            outward[1].forward()
+            outward[2].through()
+            outward[1].column()
         totals = sum_finish(step, ar)
         if step == 0:
             norm_now = totals[3:4]
         alpha = norm_now / totals[0:1]
-        norm_next = jnp.maximum(norm_now - 2.0 * alpha * totals[1:2] + alpha * alpha * totals[2:3], 0.0)
         coef[2 * step] = as_rows(alpha)
-        coef[2 * step + 1] = as_rows(norm_next / norm_now)
-        norm_now = norm_next
-
-    arrived(planes[2])
-    forwards[2] = forward_start(g_vec[3])
-    arrived(forwards[2])
-    columns[2] = column_start(g_vec[3], zs_vec.at[3], zr_vec.at[3], 1)
-    for step in range(3):
-        arrived(columns[step])
-    images = [column_sum(zr_vec.at[step + 1]) for step in range(3)]
-    for half in range(2):
-        lanes = pl.ds(half * BLOCK, BLOCK)
-        residual = direction = right_ref[:, lanes]
-        total = jnp.zeros_like(residual)
-        for step in range(3):
-            total = total + coef[2 * step] * direction
-            residual = residual - coef[2 * step] * (nugget * direction + images[step][half])
-            if step < 2:
-                direction = residual + coef[2 * step + 1] * direction
-        solution_ref[:, lanes] = total
-        residual_ref[:, lanes] = residual
+        if step < 2:
+            norm_next = norm_now - 2.0 * alpha * totals[1:2] + alpha * alpha * totals[2:3]
+            norm_next = jnp.maximum(norm_next, 0.0)
+            coef[2 * step + 1] = as_rows(norm_next / norm_now)
+            norm_now = norm_next
+
+    images = [outward[step].sums(0) for step in range(2)]
+    for ch in range(CHUNKS[3]):
+        last = outward[2].sums(ch)
+        rows = rows_of(3, ch)
+        size = R // CHUNKS[3]
+        cut = slice(ch * size, (ch + 1) * size)
+        for half in range(2):
+            lanes = pl.ds(half * BLOCK, BLOCK)
+            residual = direction = right_ref[rows, lanes]
+            total = jnp.zeros_like(residual)
+            for step in range(3):
+                image = last[half] if step == 2 else images[step][half][cut]
+                total = total + coef[2 * step, rows, :] * direction
+                residual = residual - coef[2 * step, rows, :] * (nugget * direction + image)
+                if step < 2:
+                    direction = residual + coef[2 * step + 1, rows, :] * direction
+            solution_ref[rows, lanes] = total
+            residual_ref[rows, lanes] = residual
 
     assert len(phases) == PHASES
     for phase, view in enumerate(phases):
@@ -380,13 +404,13 @@
         in_specs=[vmem, vmem],
         out_specs=(vmem, vmem),
         scratch_shapes=[
+            *[pltpu.VMEM((4 * chips + 1, R // n, BLOCK), bf16) for n in CHUNKS for _ in range(n)],
+            *[pltpu.VMEM((n, 2 * depth, R // n, BLOCK), bf16) for n in CHUNKS],
+            *[pltpu.VMEM((n, 2 * depth, R // n, BLOCK), bf16) for n in CHUNKS],
             pltpu.VMEM((4 * chips + 1, 8, BLOCK), f32),
-            *[pltpu.VMEM((4 * chips + 1, R, BLOCK), bf16)] * 4,
             pltpu.VMEM((2 * depth, 8, BLOCK), f32),
             pltpu.VMEM((2 * depth, 8, BLOCK), f32),
             pltpu.VMEM((2 * depth, 8, BLOCK), f32),
-            pltpu.VMEM((4, 2 * depth, R, BLOCK), bf16),
-            pltpu.VMEM((4, 2 * depth, R, BLOCK), bf16),
             pltpu.VMEM((36, 8, BLOCK), f32),
             pltpu.VMEM((3, 36, R, BLOCK), bf16),
             pltpu.VMEM((9, 4 * BLOCK, 2 * BLOCK), bf16),

time: 110 us -> 89.8 us (0.82)
  Pallas kernels: 107 us -> 86.2 us
    pallas_call x1, Pallas kernels: 107 us -> 86.2 us  [per_device(): pl.pallas_call(functools.partial(kernel, side, depth), out_shape=(out, ou...]
where the time goes in v2:
time: 89.8 us; the launch traced here: 89.7 us
  Pallas kernels  86.2 us (96%)
  local copies, waits for them, and re-layouts  2.78 us (3%)
    pallas_call x1, Pallas kernels, per_device(): pl.pallas_call(functools.partial(kernel, side, depth), out_shape=(out, ou...  86.2 us
    unnamed x6, local copies, waits for them, and re-layouts  2.78 us

profile of v2, /device:TPU:1, one launch (start us, length us, event | category | flops | bytes accessed | tf_op | source)
XLA Modules:
  0.0 89.7 jit_solution(12768671483021465094)
XLA Ops:
  0.6 0.0 copy-start
  0.6 0.8 copy-done
  1.5 0.0 copy-start.1
  1.5 0.7 copy-done.1
  2.2 86.2 %shard_map.41 = (f32[64,256]{1,0:T(8,128)S(1)}, f32[64,256]{1,0:T(8,128)S(1)}) custom-call(f32[4,256]{1,0:T(4,128)S(1)} %copy-done.1, f32[64,256]{1,0:T(8,128)S(1)} %copy-done), custom_call_target="tpu_custom_call" | custom-call | tf_op jit(solution)/shard_map/pallas_call | solution.py:401
  88.4 0.6 copy.6
  89.0 0.6 copy.7
Async XLA Ops:
  0.6 0.8 copy-start
  1.5 0.7 copy-start.1

commit v3 on v2

--- a/solution.py
+++ b/solution.py
@@ -29,16 +29,16 @@
     return sj * (wendland(d * (1.0 / long_range)) + wendland(d * (1.0 / short_range))) * si
 
 
-def kernel(side, depth, point_ref, right_ref, solution_ref, residual_ref, *scratch):
+def kernel(side, depth, point_hbm, right_hbm, solution_ref, residual_ref, *scratch):
     chips = side * side
     slots = 4 * chips
     zslots = 2 * depth
-    R = right_ref.shape[0]
+    R = right_hbm.shape[0]
     g_vec = [list(scratch[sum(CHUNKS[:v]):sum(CHUNKS[:v + 1])]) for v in range(4)]
     zs_vec = scratch[sum(CHUNKS):sum(CHUNKS) + 4]
     zr_vec = scratch[sum(CHUNKS) + 4:sum(CHUNKS) + 8]
     (g_pts, line_pts, zs_pts, zr_pts, h_pts, h_vec, tiles, p_all, r_all, ar_one, ar_two,
-     table_v, table_s, coef, send, recv, local_sem) = scratch[sum(CHUNKS) + 8:]
+     table_v, table_s, coef, point_ref, right_ref, send, recv, local_sem) = scratch[sum(CHUNKS) + 8:]
     my_z = lax.axis_index("row")
     my_col = lax.axis_index("col")
     core = my_col % 2
@@ -169,6 +169,22 @@
             arrived(self.columns[ch])
             return column_sum(zr_vec[self.v].at[ch])
 
+    load = [
+        pltpu.make_async_copy(point_hbm, point_ref, local_sem.at[0]),
+        pltpu.make_async_copy(right_hbm, right_ref, local_sem.at[1]),
+    ]
+    for copy in load:
+        copy.start()
+
+    barrier = pltpu.get_barrier_semaphore()
+
+    def greet(peer):
+        pl.semaphore_signal(barrier, inc=1, device_id=peer, device_id_type=MESH)
+
+    loop(1, chips, lambda o: greet(plane_peer(o)))
+    loop(1, depth, lambda o: greet(line_peer(o)))
+    greet(sibling)
+    load[0].wait()
     pts = point_ref[...]
     for half in range(2):
         here = pts[:, half * BLOCK:(half + 1) * BLOCK]
@@ -186,6 +202,8 @@
         g_pts[own + half, 5:6, :] = slot
         g_pts[own + half, 6:7, :] = slab
         line_pts[2 * my_z + half] = g_pts[own + half]
+    load[1].wait()
+    for half in range(2):
         for ch in range(CHUNKS[0]):
             part = right_ref[rows_of(0, ch), half * BLOCK:(half + 1) * BLOCK]
             g_vec[0][ch][own + half] = part.astype(jnp.bfloat16)
@@ -194,14 +212,6 @@
         for buf in g_vec[v]:
             buf[slots] = jnp.zeros((R // CHUNKS[v], BLOCK), jnp.bfloat16)
 
-    barrier = pltpu.get_barrier_semaphore()
-
-    def greet(peer):
-        pl.semaphore_signal(barrier, inc=1, device_id=peer, device_id_type=MESH)
-
-    loop(1, chips, lambda o: greet(plane_peer(o)))
-    loop(1, depth, lambda o: greet(line_peer(o)))
-    greet(sibling)
     pl.semaphore_wait(barrier, chips - 1 + depth - 1 + 1)
 
     pts_plane = plane_start(g_pts)
@@ -229,7 +239,7 @@
     for k in range(slots):
         acc = jnp.minimum(acc, jnp.where(g_pts[k] == target, jnp.float32(k), gap))
     table_v[0] = jnp.clip(acc.astype(jnp.int32), 0, slots)
-    copy = pltpu.make_async_copy(table_v, table_s, local_sem)
+    copy = pltpu.make_async_copy(table_v, table_s, local_sem.at[0])
     copy.start()
     copy.wait()
 
@@ -261,7 +271,7 @@
     loop(0, 9, tile_column)
 
     eye = lax.broadcasted_iota(jnp.int32, (R, BLOCK), 0) == lax.broadcasted_iota(jnp.int32, (R, BLOCK), 1)
-    row8 = lax.broadcasted_iota(jnp.int32, (8, BLOCK), 0)
+    row4 = lax.broadcasted_iota(jnp.int32, (4, BLOCK), 0)
 
     def as_lanes(values):
         total = jnp.sum(values, axis=1, keepdims=True)
@@ -272,9 +282,9 @@
         return jnp.broadcast_to(column, (R, BLOCK))
 
     def sum_start(step, rows):
-        tile = jnp.zeros((8, BLOCK), jnp.float32)
+        tile = jnp.zeros((4, BLOCK), jnp.float32)
         for i, value in enumerate(rows):
-            tile = jnp.where(row8 == i, value, tile)
+            tile = jnp.where(row4 == i, value, tile)
         buf = ar_one.at[step]
         buf[chip] = tile
         phase = new_phase(buf.at[pl.ds(0, chips - 1)])
@@ -347,16 +357,19 @@
         ar = sum_start(step, rows)
         if step < 2:
             halo = halo_start(h_vec.at[step + 1])
-        outward.append(Journey(step + 1, 1))
-        if step == 1:
-            outward[0].forward()
+        if step == 2:
+            outward.append(Journey(3, 1))
+        if step > 0:
+            outward[step - 1].forward()
+        if step == 2:
+            outward[1].column()
         ar = sum_second(step, ar)
         if step == 1:
             outward[0].column()
-        if step == 2:
-            outward[1].forward()
+        if step < 2:
+            outward.append(Journey(step + 1, 1))
+        else:
             outward[2].through()
-            outward[1].column()
         totals = sum_finish(step, ar)
         if step == 0:
             norm_now = totals[3:4]
@@ -401,7 +414,7 @@
     return pl.pallas_call(
         functools.partial(kernel, side, depth),
         out_shape=(out, out),
-        in_specs=[vmem, vmem],
+        in_specs=[pl.BlockSpec(memory_space=pltpu.HBM)] * 2,
         out_specs=(vmem, vmem),
         scratch_shapes=[
             *[pltpu.VMEM((4 * chips + 1, R // n, BLOCK), bf16) for n in CHUNKS for _ in range(n)],
@@ -416,14 +429,16 @@
             pltpu.VMEM((9, 4 * BLOCK, 2 * BLOCK), bf16),
             pltpu.VMEM((36, R, BLOCK), f32),
             pltpu.VMEM((36, R, BLOCK), f32),
-            pltpu.VMEM((3, chips, 8, BLOCK), f32),
-            pltpu.VMEM((3, 2 * depth, 8, BLOCK), f32),
+            pltpu.VMEM((3, chips, 4, BLOCK), f32),
+            pltpu.VMEM((3, 2 * depth, 4, BLOCK), f32),
             pltpu.VMEM((2, 8, BLOCK), jnp.int32),
             pltpu.SMEM((2, 8, BLOCK), jnp.int32),
             pltpu.VMEM((6, R, BLOCK), f32),
+            pltpu.VMEM(point_data.shape, f32),
+            pltpu.VMEM(right_side.shape, f32),
             pltpu.SemaphoreType.DMA((PHASES,)),
             pltpu.SemaphoreType.DMA((PHASES,)),
-            pltpu.SemaphoreType.DMA,
+            pltpu.SemaphoreType.DMA((2,)),
         ],
         compiler_params=pltpu.CompilerParams(
             collective_id=0, has_side_effects=True, vmem_limit_bytes=40 << 20

time: 89.8 us -> 84.5 us (0.941)
  Pallas kernels: 86.2 us -> 80.9 us
    pallas_call x1, Pallas kernels: 86.2 us -> 80.9 us  [per_device(): pl.pallas_call(functools.partial(kernel, side, depth), out_shape=(out, ou...]
where the time goes in v3:
time: 84.5 us; the launch traced here: 84.4 us
  Pallas kernels  80.9 us (96%)
  local copies, waits for them, and re-layouts  2.78 us (3%)
    pallas_call x1, Pallas kernels, per_device(): pl.pallas_call(functools.partial(kernel, side, depth), out_shape=(out, ou...  80.9 us
    unnamed x6, local copies, waits for them, and re-layouts  2.78 us

profile of v3, /device:TPU:1, one launch (start us, length us, event | category | flops | bytes accessed | tf_op | source)
XLA Modules:
  0.0 84.4 jit_solution(10425179815061679532)
XLA Ops:
  0.6 0.0 copy-start
  0.6 0.8 copy-done
  1.5 0.0 copy-start.1
  1.5 0.7 copy-done.1
  2.2 80.9 %shard_map.41 = (f32[64,256]{1,0:T(8,128)S(1)}, f32[64,256]{1,0:T(8,128)S(1)}) custom-call(f32[4,256]{1,0:T(4,128)S(1)} %copy-done.1, f32[64,256]{1,0:T(8,128)S(1)} %copy-done), custom_call_target="tpu_custom_call" | custom-call | tf_op jit(solution)/shard_map/pallas_call | solution.py:414
  83.1 0.6 copy.6
  83.7 0.6 copy.7
Async XLA Ops:
  0.6 0.8 copy-start
  1.5 0.7 copy-start.1

commit v4 on v3

--- a/solution.py
+++ b/solution.py
@@ -361,11 +361,9 @@
             outward.append(Journey(3, 1))
         if step > 0:
             outward[step - 1].forward()
-        if step == 2:
-            outward[1].column()
         ar = sum_second(step, ar)
-        if step == 1:
-            outward[0].column()
+        if step > 0:
+            outward[step - 1].column()
         if step < 2:
             outward.append(Journey(step + 1, 1))
         else:

time: 84.5 us -> 84 us (level)
  no operation moved by 1% of the time
where the time goes in v4:
time: 84 us; the launch traced here: 83.8 us
  Pallas kernels  80.4 us (96%)
  local copies, waits for them, and re-layouts  2.78 us (3%)
    pallas_call x1, Pallas kernels, per_device(): pl.pallas_call(functools.partial(kernel, side, depth), out_shape=(out, ou...  80.4 us
    unnamed x6, local copies, waits for them, and re-layouts  2.78 us

profile of v4, /device:TPU:1, one launch (start us, length us, event | category | flops | bytes accessed | tf_op | source)
XLA Modules:
  0.0 83.8 jit_solution(17708322139909372400)
XLA Ops:
  0.6 0.0 copy-start
  0.6 0.8 copy-done
  1.5 0.0 copy-start.1
  1.5 0.7 copy-done.1
  2.2 80.4 %shard_map.41 = (f32[64,256]{1,0:T(8,128)S(1)}, f32[64,256]{1,0:T(8,128)S(1)}) custom-call(f32[4,256]{1,0:T(4,128)S(1)} %copy-done.1, f32[64,256]{1,0:T(8,128)S(1)} %copy-done), custom_call_target="tpu_custom_call" | custom-call | tf_op jit(solution)/shard_map/pallas_call | solution.py:412
  82.5 0.6 copy.6
  83.2 0.6 copy.7
Async XLA Ops:
  0.6 0.8 %copy-start = (f32[64,256]{1,0:T(8,128)S(1)}, f32[64,256]{1,0:T(8,128)}, u32[]{:S(2)}) copy-start(f32[64,256]{1,0:T(8,128)} %right_hbm.1) | copy-start | bytes 196612
  1.5 0.7 copy-start.1

commit v5 on v4

--- a/solution.py
+++ b/solution.py
@@ -439,7 +439,7 @@
             pltpu.SemaphoreType.DMA((2,)),
         ],
         compiler_params=pltpu.CompilerParams(
-            collective_id=0, has_side_effects=True, vmem_limit_bytes=40 << 20
+            collective_id=0, has_side_effects=True, vmem_limit_bytes=55040 << 10
         ),
     )(point_data, right_side)
 

time: 84 us -> 83 us (0.988)
    unnamed x6 -> x4, local copies, waits for them, and re-layouts: 2.78 us -> 1.94 us
where the time goes in v5:
time: 83 us; the launch traced here: 82.9 us
  Pallas kernels  80.3 us (97%)
  local copies, waits for them, and re-layouts  1.94 us (2%)
    pallas_call x1, Pallas kernels, per_device(): pl.pallas_call(functools.partial(kernel, side, depth), out_shape=(out, ou...  80.3 us
    unnamed x4, local copies, waits for them, and re-layouts  1.94 us

profile of v5, /device:TPU:1, one launch (start us, length us, event | category | flops | bytes accessed | tf_op | source)
XLA Modules:
  0.0 82.9 jit_solution(4971929882801092943)
XLA Ops:
  0.6 0.0 copy-start
  0.6 0.7 copy-done
  1.3 80.3 %shard_map.41 = (f32[64,256]{1,0:T(8,128)S(1)}, f32[64,256]{1,0:T(8,128)S(1)}) custom-call(f32[4,256]{1,0:T(4,128)S(1)} %copy-done, f32[64,256]{1,0:T(8,128)} %right_hbm.1), custom_call_target="tpu_custom_call" | custom-call | tf_op jit(solution)/shard_map/pallas_call | solution.py:412
  81.6 0.6 copy.6
  82.2 0.6 copy.7
Async XLA Ops:
  0.6 0.7 copy-start

commit v6 on v5

--- a/solution.py
+++ b/solution.py
@@ -90,15 +90,17 @@
     def loop(lo, hi, body):
         lax.fori_loop(lo, hi, lambda i, c: (body(i), c)[1], 0)
 
-    def plane_start(buf):
-        phase = new_phase(buf.at[pl.ds(0, 2 * (chips - 1))])
-        part = buf.at[pl.ds(own, 2)]
+    def plane_start(buf, rows=None):
+        rows = pl.ds(0, buf.shape[1] if rows is None else rows)
+        phase = new_phase(buf.at[pl.ds(0, 2 * (chips - 1)), rows])
+        part = buf.at[pl.ds(own, 2), rows]
         loop(1, chips, lambda o: push(part, part, phase, plane_peer(o)))
         return phase
 
-    def forward_start(buf):
-        phase = new_phase(buf.at[pl.ds(0, 2 * chips)])
-        part = buf.at[pl.ds(core * 2 * chips, 2 * chips)]
+    def forward_start(buf, rows=None):
+        rows = pl.ds(0, buf.shape[1] if rows is None else rows)
+        phase = new_phase(buf.at[pl.ds(0, 2 * chips), rows])
+        part = buf.at[pl.ds(core * 2 * chips, 2 * chips), rows]
         push(part, part, phase, sibling)
         return phase
 
@@ -184,6 +186,7 @@
     loop(1, chips, lambda o: greet(plane_peer(o)))
     loop(1, depth, lambda o: greet(line_peer(o)))
     greet(sibling)
+    g_pts[:, 5:8, :] = jnp.zeros((slots + 1, 3, BLOCK), jnp.float32)
     load[0].wait()
     pts = point_ref[...]
     for half in range(2):
@@ -214,13 +217,13 @@
 
     pl.semaphore_wait(barrier, chips - 1 + depth - 1 + 1)
 
-    pts_plane = plane_start(g_pts)
+    pts_plane = plane_start(g_pts, 5)
     line = new_phase(line_pts.at[pl.ds(0, 2 * (depth - 1))])
     mine = line_pts.at[pl.ds(2 * my_z, 2)]
     loop(1, depth, lambda o: push(mine, mine, line, line_peer(o)))
     inward = Journey(0, 0)
     arrived(pts_plane)
-    pts_forward = forward_start(g_pts)
+    pts_forward = forward_start(g_pts, 5)
     arrived(line)
 
     lane = lax.broadcasted_iota(jnp.int32, (8, BLOCK), 1)

time: 83 us -> 82.6 us (level)
  no operation moved by 1% of the time
where the time goes in v6:
time: 82.6 us; the launch traced here: 82.5 us
  Pallas kernels  79.9 us (97%)
  local copies, waits for them, and re-layouts  1.94 us (2%)
    pallas_call x1, Pallas kernels, per_device(): pl.pallas_call(functools.partial(kernel, side, depth), out_shape=(out, ou...  79.9 us
    unnamed x4, local copies, waits for them, and re-layouts  1.94 us

profile of v6, /device:TPU:1, one launch (start us, length us, event | category | flops | bytes accessed | tf_op | source)
XLA Modules:
  0.0 82.5 jit_solution(17406134427717893244)
XLA Ops:
  0.6 0.0 copy-start
  0.6 0.7 copy-done
  1.3 79.9 %shard_map.41 = (f32[64,256]{1,0:T(8,128)S(1)}, f32[64,256]{1,0:T(8,128)S(1)}) custom-call(f32[4,256]{1,0:T(4,128)S(1)} %copy-done, f32[64,256]{1,0:T(8,128)} %right_hbm.1), custom_call_target="tpu_custom_call" | custom-call | tf_op jit(solution)/shard_map/pallas_call | solution.py:415
  81.2 0.6 copy.6
  81.8 0.6 copy.7
Async XLA Ops:
  0.6 0.7 copy-start
